TPU v7x, 32 devices: a whole 2x2x4 slice. The times are simulated.
32 devices in a mesh: groups: 2 (over x), depth: 8 (over z, y), height: 2 (over core).
Axes of the slice: x: 2, y: 2, z: 4, core: 2. Of those that a mesh axis runs over, the one named last changes fastest.
Arguments:
- images: bfloat16 [4, 4, 64, 16, 256], P('groups', None, 'depth', 'height'), parts along dimension 0, may hold values from -6 to 6
- pre_hidden: bfloat16 [4, 16, 64, 16, 256], P('groups', None, 'depth', 'height'), parts along dimension 0, may hold values from -6 to 6
- pre_deep: bfloat16 [4, 32, 32, 8, 128], P(('groups', 'height'), None, 'depth'), parts along dimension 0, may hold values from -6 to 6
- pooled_grad: bfloat16 [4, 32, 16, 256], P(('groups', 'height'), None, 'depth'), parts along dimension 0, may hold values from -1.25 to 1.25
- deep_weight: bfloat16 [32, 16, 3, 3, 3], replicated, may hold values from -0.3125 to 0.3125
Outputs:
- first_kernel: float32 [32, 4, 3, 3, 3], P('groups'), parts along dimension 0
- first_bias: float32 [32], P('groups'), parts along dimension 0
- deep_kernel: float32 [64, 16, 3, 3, 3], P('groups'), parts along dimension 0
- deep_bias: float32 [64], P('groups'), parts along dimension 0
There are 2 independent parts, one for each index of `groups`. A program takes and returns all parts, laid end to end along the dimension named above; an argument that names none is the same for every part. Nothing has to cross between parts.
All inputs are finite; a program needn't handle non-finite values.
Results may differ from a plain program's by a relative error of at most 0.0031.
Values may be sent and summed in bfloat16 or wider, within the bound.
A program may use at most 128 MiB of HBM per device.

v0:
```python
import jax
import jax.numpy as jnp
from jax import lax
from jax.sharding import PartitionSpec as P

SLOPE = 0.3


def padded_2(block, sides, width):
    for axis, dim in sides:
        count = lax.axis_size(axis)
        forward = [(i, i + 1) for i in range(count - 1)]
        backward = [(target, source) for source, target in forward]
        low = lax.ppermute(
            lax.slice_in_dim(block, block.shape[dim] - width, None, axis=dim), axis, forward
        )
        high = lax.ppermute(lax.slice_in_dim(block, 0, width, axis=dim), axis, backward)
        block = jnp.concatenate([low, block, high], axis=dim)
    return block


def from_behind(value, axis, steps):
    count = lax.axis_size(axis)
    leading, last = (max(0, -steps), min(count, count - steps))
    return lax.ppermute(value, axis, [(source, source + steps) for source in range(leading, last)])


def leaky(values):
    return jnp.where(values > 0, values, SLOPE * values)


def slope_at(values):
    return jnp.where(values > 0, 1.0, SLOPE)


def deep_gradient(pooled_grad, pre_deep):
    samples, chans, quarter, flat = pooled_grad.shape
    half_depth, half_height, half_width = (pre_deep.shape[2], pre_deep.shape[3], pre_deep.shape[4])
    coarse = (
        pooled_grad.astype(jnp.float32).reshape(
            samples, chans, quarter, 1, half_height // 2, 1, half_width // 2, 1
        )
        / 8.0
    )
    spread = jnp.broadcast_to(
        coarse, (samples, chans, quarter, 2, half_height // 2, 2, half_width // 2, 2)
    )
    spread = spread.reshape(samples, chans, half_depth, half_height, half_width)
    return (spread * slope_at(pre_deep.astype(jnp.float32))).astype(jnp.bfloat16)


def deep_weight_grad(local_grad, padded):
    samples, chans = (padded.shape[0], padded.shape[1])
    coarse_depth, coarse_height, coarse_width = (
        local_grad.shape[2],
        local_grad.shape[3],
        local_grad.shape[4],
    )
    grown = jnp.pad(padded, ((0, 0), (0, 0), (0, 1), (0, 1), (0, 1)))
    phases = grown.reshape(
        samples, chans, coarse_depth + 1, 2, coarse_height + 1, 2, coarse_width + 1, 2
    )
    phases = phases.transpose(0, 1, 3, 5, 7, 2, 4, 6)
    kernels = []
    for depth_tap in range(3):
        for height_tap in range(3):
            for width_tap in range(3):
                depth_off, height_off, width_off = (depth_tap // 2, height_tap // 2, width_tap // 2)
                view = phases[
                    :,
                    :,
                    depth_tap % 2,
                    height_tap % 2,
                    width_tap % 2,
                    depth_off : depth_off + coarse_depth,
                    height_off : height_off + coarse_height,
                    width_off : width_off + coarse_width,
                ]
                kernels.append(
                    jnp.einsum(
                        "sodhw,sidhw->oi", local_grad, view, preferred_element_type=jnp.float32
                    )
                )
    kernel = jnp.stack(kernels, axis=-1).reshape(local_grad.shape[1], chans, 3, 3, 3)
    return (kernel, jnp.sum(local_grad, axis=(0, 2, 3, 4), dtype=jnp.float32))


def transpose_conv(extended, deep_weight):
    samples = extended.shape[0]
    coarse_depth, coarse_height, coarse_width = (
        extended.shape[2] - 1,
        extended.shape[3] - 1,
        extended.shape[4] - 1,
    )
    out_chans = deep_weight.shape[1]
    phase_taps = (((1, 0),), ((2, 0), (0, 1)))
    phases = []
    for depth_phase in range(2):
        for height_phase in range(2):
            for width_phase in range(2):
                views = []
                mats = []
                for depth_tap, depth_step in phase_taps[depth_phase]:
                    for height_tap, height_step in phase_taps[height_phase]:
                        for width_tap, width_step in phase_taps[width_phase]:
                            views.append(
                                extended[
                                    :,
                                    :,
                                    depth_step : depth_step + coarse_depth,
                                    height_step : height_step + coarse_height,
                                    width_step : width_step + coarse_width,
                                ]
                            )
                            mats.append(deep_weight[:, :, depth_tap, height_tap, width_tap])
                stacked = jnp.concatenate(views, axis=1)
                matrix = jnp.concatenate(mats, axis=0)
                phases.append(
                    jnp.einsum(
                        "sodhw,oi->sidhw", stacked, matrix, preferred_element_type=jnp.float32
                    )
                )
    grid = jnp.stack(phases, axis=0).reshape(
        2, 2, 2, samples, out_chans, coarse_depth, coarse_height, coarse_width
    )
    woven = grid.transpose(3, 4, 5, 0, 6, 1, 7, 2).reshape(
        samples, out_chans, 2 * coarse_depth, 2 * coarse_height, 2 * coarse_width
    )
    return woven.astype(jnp.bfloat16)


def first_weight_grad(first_grad, framed):
    chans = framed.shape[1]
    cells_depth, cells_height, cells_width = (
        first_grad.shape[2],
        first_grad.shape[3],
        first_grad.shape[4],
    )
    kernels = []
    for depth_tap in range(3):
        for height_tap in range(3):
            for width_tap in range(3):
                view = framed[
                    :,
                    :,
                    depth_tap : depth_tap + cells_depth,
                    height_tap : height_tap + cells_height,
                    width_tap : width_tap + cells_width,
                ]
                kernels.append(
                    jnp.einsum(
                        "sodhw,sidhw->oi", first_grad, view, preferred_element_type=jnp.float32
                    )
                )
    kernel = jnp.stack(kernels, axis=-1).reshape(first_grad.shape[1], chans, 3, 3, 3)
    return (kernel, jnp.sum(first_grad, axis=(0, 2, 3, 4), dtype=jnp.float32))


def on_device(images, pre_hidden, pre_deep, pooled_grad, deep_weight):
    deep_grad = deep_gradient(pooled_grad, pre_deep)
    hidden = leaky(pre_hidden.astype(jnp.float32)).astype(jnp.bfloat16)
    bordered = padded_2(images, (("depth", 2), ("height", 3)), 1)
    framed = jnp.pad(bordered, ((0, 0), (0, 0), (0, 0), (0, 0), (1, 1)))
    gathered = lax.all_to_all(hidden, "height", split_axis=0, concat_axis=3, tiled=True)
    below = from_behind(gathered[:, :, -1:], "depth", 1)
    padded = jnp.pad(
        jnp.concatenate([below, gathered], axis=2), ((0, 0), (0, 0), (0, 0), (1, 0), (1, 0))
    )
    above = from_behind(deep_grad[:, :, :1], "depth", -1)
    extended = jnp.pad(
        jnp.concatenate([deep_grad, above], axis=2), ((0, 0), (0, 0), (0, 0), (0, 1), (0, 1))
    )
    returned = transpose_conv(extended, deep_weight)
    hidden_grad = lax.all_to_all(returned, "height", split_axis=3, concat_axis=0, tiled=True)
    deep_kernel, deep_bias = deep_weight_grad(deep_grad, padded)
    first_grad = (
        hidden_grad.astype(jnp.float32) * slope_at(pre_hidden.astype(jnp.float32))
    ).astype(jnp.bfloat16)
    first_kernel, first_bias = first_weight_grad(first_grad, framed)
    first_kernel, first_bias, deep_kernel, deep_bias = lax.psum(
        (first_kernel, first_bias, deep_kernel, deep_bias), ("depth", "height")
    )
    return (first_kernel, first_bias, deep_kernel, deep_bias)


def solution(mesh):
    return jax.shard_map(
        on_device,
        mesh=mesh,
        in_specs=(
            P("groups", None, "depth", "height", None),
            P("groups", None, "depth", "height", None),
            P(("groups", "height"), None, "depth", None, None),
            P(("groups", "height"), None, "depth", None),
            P(),
        ),
        out_specs=(
            P("groups", None, None, None, None),
            P("groups"),
            P("groups", None, None, None, None),
            P("groups"),
        ),
        check_vma=False,
    )
```

profile of v0, /device:TPU:0, one launch (start us, length us, event | category | flops | bytes accessed | tf_op | source)
XLA Modules:
  0.0 230.6 jit_solution(8759666628445355263)
XLA Ops:
  0.6 1.2 copy.92
  2.5 1.3 collective-permute-start.2
  3.8 6.1 %collective-permute-start.1 = (bf16[2,4,1,8,256]{4,1,0,3,2:T(4,128)(2,1)}, bf16[2,4,1,8,256]{4,1,0,3,2:T(4,128)(2,1)}, u32[]{:S(2)}, u32[]{:S(2)}) collective-permute-start(bf16[2,4,1,8,256]{4,1,0,3,2:T(4,128)(2,1)} %get-tuple-element.24), channel_id=1, source_target_pairs={{0,2},{2,4},{4,6},{6,8},{8,10},{10,12},{12,14},{1,3},{3,5},{5,7},{... | collective-permute-start | bytes 98312 | tf_op jit(solution)/shard_map/ppermute | solution.py:14
  10.9 0.9 broadcast_in_dim.23
  13.2 1.3 collective-permute-start
  18.3 1.2 constant_dynamic-update-slice_fusion.8
  21.0 2.1 collective-permute-start.3
  23.0 1.3 collective-permute-start.4
  28.2 14.3 %copy.88 = bf16[2,2,2,1,16,4,8,128]{4,2,7,1,6,0,5,3:T(2,128)(2,1)} copy(bf16[2,2,2,1,16,4,8,128]{7,4,6,5,2,1,0,3:T(8,128)(2,1)S(1)} %bitcast.783) | data formatting | bytes 2097152 | tf_op jit(solution)/shard_map/convert_element_type | solution.py:129
  42.5 6.9 %copy.89 = bf16[1,16,8,16,256]{4,2,1,0,3:T(8,128)(2,1)S(1)} copy(bf16[1,16,8,16,256]{1,4,3,2,0:T(8,128)(2,1)} %bitcast.752) | data formatting | bytes 2097152 | tf_op jit(solution)/shard_map/convert_element_type | solution.py:129
  49.4 5.9 %all_to_all.27 = bf16[1,16,8,16,256]{4,2,1,0,3:T(8,128)(2,1)S(1)} all-to-all(bf16[1,16,8,16,256]{4,2,1,0,3:T(8,128)(2,1)S(1)} %copy.89), channel_id=1, replica_groups=mesh['groups'=2,'depth'=8,'height'=2] {'height'}, dimensions={3} | all-to-all | bytes 2097152 | tf_op jit(solution)/shard_map/all_to_all | solution.py:174
  55.3 1.3 convert_reduce_fusion
  56.8 4.7 %all_to_all.28 = bf16[2,16,8,8,256]{4,3,2,1,0:T(8,128)(2,1)S(1)} all-to-all(bf16[2,16,8,8,256]{4,3,2,1,0:T(8,128)(2,1)S(1)} %copy.125), channel_id=1, replica_groups=mesh['groups'=2,'depth'=8,'height'=2] {'height'}, dimensions={0} | all-to-all | bytes 2097152 | tf_op jit(solution)/shard_map/all_to_all | solution.py:164
  61.6 4.9 %collective-permute-start.5 = (bf16[1,16,1,16,256]{4,3,2,1,0:T(8,128)(2,1)S(1)}, bf16[1,16,1,16,256]{4,3,2,1,0:T(8,128)(2,1)S(1)}, u32[]{:S(2)}, u32[]{:S(2)}) collective-permute-start(bf16[1,16,1,16,256]{4,3,2,1,0:T(8,128)(2,1)S(1)} %slice.448), channel_id=1, source_target_pairs={{0,2},{2,4},{4,6},{6,8},{8,10},{10,12},{12,14},{1,3},{3,5},{5,7},{... | collective-permute-start | bytes 393224 | tf_op jit(solution)/shard_map/ppermute | solution.py:25
  66.5 1.4 select_maximum_fusion
  68.7 1.6 fusion.81
  70.3 0.9 fusion.80
  72.0 1.6 fusion.78
  75.2 1.6 fusion.75
  76.8 0.9 fusion.74
  78.5 1.6 fusion.72
  80.1 0.9 fusion.71
  81.8 0.9 fusion.69
  84.4 1.8 fusion.66
  87.9 1.6 fusion.63
  91.1 1.6 fusion.60
  94.4 1.6 fusion.57
  97.0 6.6 %copy.193 = bf16[1,16,9,16,256]{1,4,3,2,0:T(8,128)(2,1)} copy(bf16[1,16,9,16,256]{4,3,2,1,0:T(8,128)(2,1)S(1)} %pad_maximum_fusion.4) | data formatting | bytes 2359296
  103.6 10.9 %pad.82 = bf16[1,16,10,18,258]{1,4,3,2,0:T(8,128)(2,1)} pad(bf16[1,16,9,16,256]{1,4,3,2,0:T(8,128)(2,1)} %copy.193, bf16[]{:T(256)} %constant.3.clone.1), padding=0_0x0_0x0_1x1_1x1_1 | pad | bytes 2665730 | tf_op jit(solution)/shard_map/jit(_pad)/pad | solution.py:59
  114.5 24.0 %reshape.237 = bf16[1,16,5,2,9,2,129,2]{1,7,6,5,4,3,2,0:T(2,128)(2,1)} reshape(bf16[1,16,10,18,258]{1,4,3,2,0:T(8,128)(2,1)} %pad.82) | data formatting | bytes 2972160 | tf_op jit(solution)/shard_map/reshape | solution.py:60
  138.5 22.6 %copy.128 = bf16[1,16,5,2,9,2,129,2]{6,1,4,2,7,5,3,0:T(8,128)(2,1)S(1)} copy(bf16[1,16,5,2,9,2,129,2]{1,7,6,5,4,3,2,0:T(2,128)(2,1)} %reshape.237) | data formatting | bytes 2972160 | tf_op jit(solution)/shard_map/reshape | solution.py:60
  166.9 63.7 %all-reduce.4 = (f32[16,4,3,3,3]{0,1,4,3,2:T(4,128)}, f32[16]{0:T(128)}, f32[32,16,3,3,3]{0,1,4,3,2:T(8,128)}, f32[32]{0:T(128)}) all-reduce(f32[16,4,3,3,3]{0,1,4,3,2:T(4,128)S(1)} %bitcast.786, f32[16]{0:T(128)S(1)} %get-tuple-element.10, ...), channel_id=1, replica_groups=mesh['groups'=2,'depth'=8,'height'=2] {'depth','height'}, use_global_device_ids=true, to_apply=%region_0.1 | all-reduce | flops 15600 | bytes 124800 | tf_op jit(solution)/shard_map/psum | solution.py:180
  (135 shorter events, 30.4 us)
Async XLA Ops:
  1.8 8.1 %copy-start.4 = (bf16[2,4,8,8,256]{4,1,0,3,2:T(4,128)(2,1)}, bf16[2,4,8,8,256]{4,1,0,3,2:T(4,128)(2,1)S(1)}, u32[]{:S(2)}) copy-start(bf16[2,4,8,8,256]{4,1,0,3,2:T(4,128)(2,1)S(1)} %copy.92) | copy-start | bytes 786436
  2.5 16.9 %collective-permute-start.2 = (bf16[2,4,1,8,256]{4,1,0,3,2:T(4,128)(2,1)}, bf16[2,4,1,8,256]{4,1,0,3,2:T(4,128)(2,1)}, u32[]{:S(2)}, u32[]{:S(2)}) collective-permute-start(bf16[2,4,1,8,256]{4,1,0,3,2:T(4,128)(2,1)} %get-tuple-element.23), channel_id=1, source_target_pairs={{2,0},{4,2},{6,4},{8,6},{10,8},{12,10},{14,12},{3,1},{5,3},{7,5},{... | collective-permute-start | bytes 98312 | tf_op jit(solution)/shard_map/ppermute | solution.py:17
  3.8 13.7 %collective-permute-start.1 = (bf16[2,4,1,8,256]{4,1,0,3,2:T(4,128)(2,1)}, bf16[2,4,1,8,256]{4,1,0,3,2:T(4,128)(2,1)}, u32[]{:S(2)}, u32[]{:S(2)}) collective-permute-start(bf16[2,4,1,8,256]{4,1,0,3,2:T(4,128)(2,1)} %get-tuple-element.24), channel_id=1, source_target_pairs={{0,2},{2,4},{4,6},{6,8},{8,10},{10,12},{12,14},{1,3},{3,5},{5,7},{... | collective-permute-start | bytes 98312 | tf_op jit(solution)/shard_map/ppermute | solution.py:14
  10.9 1.5 copy-start.6
  11.8 2.7 %copy-start.7 = (bf16[32,16,3,3,3]{0,1,4,3,2:T(8,128)(2,1)S(1)}, bf16[32,16,3,3,3]{0,1,4,3,2:T(8,128)(2,1)}, u32[]{:S(2)}) copy-start(bf16[32,16,3,3,3]{0,1,4,3,2:T(8,128)(2,1)} %param.9) | copy-start | bytes 82948
  13.2 11.2 %collective-permute-start = (bf16[1,32,1,8,128]{4,1,3,2,0:T(8,128)(2,1)S(1)}, bf16[1,32,1,8,128]{4,1,3,2,0:T(8,128)(2,1)S(1)}, u32[]{:S(2)}, u32[]{:S(2)}) collective-permute-start(bf16[1,32,1,8,128]{4,1,3,2,0:T(8,128)(2,1)S(1)} %slice.415), channel_id=1, source_target_pairs={{2,0},{4,2},{6,4},{8,6},{10,8},{12,10},{14,12},{3,1},{5,3},{7,5},{... | collective-permute-start | bytes 196616 | tf_op jit(solution)/shard_map/ppermute | solution.py:25
  20.2 4.9 %copy-start.2 = (bf16[2,4,10,8,256]{4,1,0,3,2:T(4,128)(2,1)}, bf16[2,4,10,8,256]{4,1,0,3,2:T(4,128)(2,1)S(1)}, u32[]{:S(2)}) copy-start(bf16[2,4,10,8,256]{4,1,0,3,2:T(4,128)(2,1)S(1)} %constant_dynamic-update-slice_fusion.7) | copy-start | bytes 983044
  21.0 45.5 %collective-permute-start.3 = (bf16[2,4,10,1,256]{4,1,0,3,2:T(4,128)(2,1)}, bf16[2,4,10,1,256]{4,1,0,3,2:T(4,128)(2,1)}, u32[]{:S(2)}, u32[]{:S(2)}) collective-permute-start(bf16[2,4,10,1,256]{4,1,0,3,2:T(4,128)(2,1)} %get-tuple-element.21), channel_id=1, source_target_pairs={{0,1},{2,3},{4,5},{6,7},{8,9},{10,11},{12,13},{14,15},{16,17},{18,... | collective-permute-start | bytes 122888 | tf_op jit(solution)/shard_map/ppermute | solution.py:14
  23.0 43.5 %collective-permute-start.4 = (bf16[2,4,10,1,256]{4,1,0,3,2:T(4,128)(2,1)}, bf16[2,4,10,1,256]{4,1,0,3,2:T(4,128)(2,1)}, u32[]{:S(2)}, u32[]{:S(2)}) collective-permute-start(bf16[2,4,10,1,256]{4,1,0,3,2:T(4,128)(2,1)} %get-tuple-element.22), channel_id=1, source_target_pairs={{1,0},{3,2},{5,4},{7,6},{9,8},{11,10},{13,12},{15,14},{17,16},{19,... | collective-permute-start | bytes 122888 | tf_op jit(solution)/shard_map/ppermute | solution.py:17
  24.8 0.9 copy-start.12
  24.8 0.9 copy-start.13
  24.9 1.1 copy-start.10
  24.9 1.1 copy-start.11
  25.1 1.2 copy-start.8
  25.2 1.2 copy-start.9
  25.2 1.2 copy-start.24
  25.2 1.2 copy-start.25
  26.0 0.7 copy-start.22
  26.1 0.7 copy-start.23
  26.4 0.7 copy-start.18
  26.4 0.7 copy-start.19
  26.4 0.7 copy-start.20
  26.4 0.7 copy-start.21
  26.8 0.7 copy-start.14
  26.8 0.7 copy-start.15
  26.8 0.7 copy-start.16
  49.4 5.9 %copy-start = (bf16[2,16,8,8,256]{4,3,2,1,0:T(8,128)(2,1)S(1)}, bf16[2,16,8,8,256]{4,3,2,1,0:T(8,128)(2,1)}, u32[]{:S(2)}) copy-start(bf16[2,16,8,8,256]{4,3,2,1,0:T(8,128)(2,1)} %param.6) | copy-start | bytes 3145732
  56.8 9.7 %copy-start.3 = (bf16[2,4,10,8,256]{4,1,0,3,2:T(4,128)(2,1)S(1)}, bf16[2,4,10,8,256]{4,1,0,3,2:T(4,128)(2,1)}, u32[]{:S(2)}) copy-start(bf16[2,4,10,8,256]{4,1,0,3,2:T(4,128)(2,1)} %copy-done.2) | copy-start | bytes 983044
  61.6 35.3 %collective-permute-start.5 = (bf16[1,16,1,16,256]{4,3,2,1,0:T(8,128)(2,1)S(1)}, bf16[1,16,1,16,256]{4,3,2,1,0:T(8,128)(2,1)S(1)}, u32[]{:S(2)}, u32[]{:S(2)}) collective-permute-start(bf16[1,16,1,16,256]{4,3,2,1,0:T(8,128)(2,1)S(1)} %slice.448), channel_id=1, source_target_pairs={{0,2},{2,4},{4,6},{6,8},{8,10},{10,12},{12,14},{1,3},{3,5},{5,7},{... | collective-permute-start | bytes 393224 | tf_op jit(solution)/shard_map/ppermute | solution.py:25
  70.3 1.7 copy-start.5
  80.1 1.7 copy-start.1
  164.7 2.2 copy-start.26
  (1 other events, 0.7 us)
where the time goes:
time: 233 us; the launch traced here: 231 us
  local copies, waits for them, and re-layouts  95.9 us (41%)
  blocking collectives  74.3 us (32%)
  matrix products  37.7 us (16%)
  starting transfers between devices  16.9 us (7%)
  other arithmetic  4.49 us (2%)
    psum x1, blocking collectives, on_device(): lax.psum((first_kernel, first_bias, deep_kernel, deep_bias), ('depth', 'h...  63.7 us
    reshape x2, local copies, waits for them, and re-layouts, deep_weight_grad(): grown.reshape(samples, chans, coarse_depth + 1, 2, coarse_height + 1, 2,...  46.6 us
    dot_general x27, matrix products, first_weight_grad(): jnp.einsum('sodhw,sidhw->oi', first_grad, view, preferred_element_type=jn...  29 us
    convert_element_type x2, local copies, waits for them, and re-layouts, transpose_conv(): return woven.astype(jnp.bfloat16)  21.2 us
    pad x1, local copies, waits for them, and re-layouts, deep_weight_grad(): grown = jnp.pad(padded, ((0, 0), (0, 0), (0, 1), (0, 1), (0, 1)))  10.9 us
    unnamed x64, local copies, waits for them, and re-layouts  10.4 us
    ppermute x2, starting transfers between devices, padded_2(): lax.ppermute(lax.slice_in_dim(block, block.shape[dim] - width, None, axis...  8.18 us
    ppermute x2, starting transfers between devices, from_behind(): lax.ppermute(value, axis, [(source, source + steps) for source in range(l...  6.15 us
  transfers between devices with their start and end apart: 6, of which 0 were waited for; matrix products, arithmetic and copies ran while one was open for 29% of the time, Pallas kernels for 0%

commit v1 on v0

v1 whole, which is shorter than its diff:
```python
import functools

import jax
import jax.numpy as jnp
from jax import lax
from jax.experimental import pallas as pl
from jax.experimental.pallas import tpu as pltpu
from jax.sharding import PartitionSpec as P

SLOPE = 0.3
MESH = pl.DeviceIdType.MESH
BF = jnp.bfloat16
F32 = jnp.float32
TAP = ((1, 1), (0, 0), (0, 1))


def vmem():
    return pl.BlockSpec(memory_space=pltpu.VMEM)


def iota(shape, dim):
    return lax.broadcasted_iota(jnp.int32, shape, dim)


def one_hot(row_target, shape):
    return jnp.where(row_target == iota(shape, 1), 1.0, 0.0).astype(BF)


def dot(a, b):
    return jnp.dot(a, b, preferred_element_type=F32)


def dot_nt(a, b):
    return lax.dot_general(a, b, (((1,), (1,)), ((), ())), preferred_element_type=F32)


def exchange_kernel(count, img, pd, pool, img_all, pd_all, pool_all, send, recv):
    k = lax.axis_index("depth")
    h = lax.axis_index("height")
    cells = img.shape[2]
    quarter = pd.shape[1]
    barrier = pltpu.get_barrier_semaphore()

    def greet(depth, height):
        pl.semaphore_signal(
            barrier, inc=1, device_id={"depth": depth, "height": height}, device_id_type=MESH
        )

    greet(k, 1 - h)

    @pl.when(k > 0)
    def _():
        greet(k - 1, 0)
        greet(k - 1, 1)

    @pl.when(k < count - 1)
    def _():
        greet(k + 1, 0)
        greet(k + 1, 1)

    pl.semaphore_wait(barrier, 1 + 2 * ((k + count - 1) // count + (2 * count - 2 - k) // count))

    def copy(src, dst, send_slot, recv_slot, depth, height):
        return pltpu.make_async_remote_copy(
            src_ref=src,
            dst_ref=dst,
            send_sem=send.at[send_slot],
            recv_sem=recv.at[recv_slot],
            device_id={"depth": depth, "height": height},
            device_id_type=MESH,
        )

    def partner(slot):
        return [
            copy(pd, pd_all.at[slot, :, 0:quarter], 0, 0, k, 1 - h),
            copy(pool, pool_all.at[slot, 0], 1, 1, k, 1 - h),
            copy(img, img_all.at[slot, :, :, 1 : cells + 1], 2, 2, k, 1 - h),
        ]

    def down(slot, height):
        base = 3 + 3 * height
        arrive = 3 + 3 * slot
        return [
            copy(pd.at[:, 0:1], pd_all.at[slot, :, quarter : quarter + 1], base, arrive, k - 1, height),
            copy(pool, pool_all.at[slot, 1], base + 1, arrive + 1, k - 1, height),
            copy(img.at[:, :, 0:1], img_all.at[slot, :, :, cells + 1 : cells + 2], base + 2, arrive + 2, k - 1, height),
        ]

    def up(slot, height):
        return [
            copy(img.at[:, :, cells - 1 : cells], img_all.at[slot, :, :, 0:1], 9 + height, 9 + slot, k + 1, height)
        ]

    @pl.when(k > 0)
    def _():
        for height in range(2):
            for c in down(h, height):
                c.start()

    @pl.when(k < count - 1)
    def _():
        for height in range(2):
            for c in up(h, height):
                c.start()

    for c in partner(h):
        c.start()
    img_all[h, :, :, 1 : cells + 1] = img[...]
    pd_all[h, :, 0:quarter] = pd[...]
    pool_all[h, 0] = pool[...]

    @pl.when(k == 0)
    def _():
        img_all[:, :, :, 0:1] = jnp.zeros_like(img_all[:, :, :, 0:1])

    @pl.when(k == count - 1)
    def _():
        img_all[:, :, :, cells + 1 : cells + 2] = jnp.zeros_like(img_all[:, :, :, 0:1])
        pd_all[:, :, quarter : quarter + 1] = jnp.zeros_like(pd_all[:, :, 0:1])
        pool_all[:, 1] = jnp.zeros_like(pool_all[:, 1])

    for c in partner(h):
        c.wait_send()
    for c in partner(1 - h):
        c.wait_recv()

    @pl.when(k > 0)
    def _():
        for height in range(2):
            for c in down(h, height):
                c.wait_send()
            for c in up(height, height):
                c.wait_recv()

    @pl.when(k < count - 1)
    def _():
        for height in range(2):
            for c in up(h, height):
                c.wait_send()
            for c in down(height, height):
                c.wait_recv()


def exchange(count, images, pre_deep, pooled):
    samples, chans, cells, rows, width = images.shape
    out_chans, coarse, coarse_rows, coarse_width = pre_deep.shape
    return pl.pallas_call(
        functools.partial(exchange_kernel, count),
        out_shape=(
            jax.ShapeDtypeStruct((2, samples, chans, cells + 2, rows, width), BF),
            jax.ShapeDtypeStruct((2, out_chans, coarse + 1, coarse_rows, coarse_width), BF),
            jax.ShapeDtypeStruct((2, 2) + pooled.shape, BF),
        ),
        in_specs=[vmem()] * 3,
        out_specs=(vmem(),) * 3,
        scratch_shapes=[pltpu.SemaphoreType.DMA((11,)), pltpu.SemaphoreType.DMA((11,))],
        compiler_params=pltpu.CompilerParams(collective_id=0, has_side_effects=True),
    )(images, pre_deep, pooled)


def compute_kernel(hid, img, pd, pool, weight, out, ph_buf, g_buf, i_buf):
    me = lax.axis_index("height")

    def cell(s, d2, h2):
        at = ((s * 4 + d2) * 4 + h2) * 128
        return slice(at, at + 128)

    row = iota((128, 128), 0)
    order = one_hot((row & 15) * 8 + (row >> 4), (128, 128))
    z = iota((256, 256), 0)
    col = iota((256, 256), 1)
    split = jnp.where(z == 2 * (col & 127) + (col >> 7), 1.0, 0.0).astype(BF)
    for s in range(2):
        for d in range(8):
            x = hid[s, :, d].astype(F32).reshape(128, 256).astype(BF)
            a = dot(x, split).astype(BF)
            b = dot(order, a).astype(BF)
            for h2 in range(4):
                for pw in range(2):
                    r = (d % 2) * 64 + pw * 32
                    ph_buf[r : r + 32, cell(s, d // 2, h2)] = b[
                        h2 * 32 : h2 * 32 + 32, pw * 128 : pw * 128 + 128
                    ]

    row = iota((160, 256), 0)
    high = 4 * me + (row >> 5)
    pick = one_hot(jnp.where(high < 8, (row & 31) * 8 + high, -1), (160, 256))
    r640 = iota((256, 640), 0)
    c640 = iota((256, 640), 1)
    spread_mat = jnp.where(
        r640 == ((4 * me + (c640 >> 7)) >> 1) * 64 + ((c640 & 127) >> 1), 1.0, 0.0
    ).astype(BF)
    lane = iota((32, 128), 1)
    deep_sum = jnp.zeros((32, 128), F32)
    for s in range(2):
        for d in range(5):
            if d % 2 == 0:
                coarse = pool[s, d // 4].astype(F32)[:, (d // 2) % 2, :].astype(BF)
                spread = dot(coarse, spread_mat) / 8.0
            x = pd[s, :, d].astype(F32).reshape(256, 128).astype(BF)
            y = dot(pick, x)
            for j in range(5):
                slope = jnp.where(y[j * 32 : j * 32 + 32] > 0, 1.0, SLOPE)
                g = (spread[:, j * 128 : j * 128 + 128] * slope).astype(BF)
                wide = g.astype(F32)
                if d < 4 and j < 4:
                    deep_sum = deep_sum + wide
                moved = jnp.where(lane < 127, pltpu.roll(wide, 127, 1), 0.0).astype(BF)
                for sd in range(2):
                    for sh in range(2):
                        if 0 <= d - sd < 4 and 0 <= j - sh < 4:
                            at = cell(s, d - sd, j - sh)
                            r = (sd * 4 + sh * 2) * 32
                            g_buf[r : r + 32, at] = g
                            g_buf[r + 32 : r + 64, at] = moved

    z = iota((256, 512), 0)
    col = iota((256, 512), 1)
    shifts = jnp.where(z == 2 * (col & 127) + (col >> 7) - 1, 1.0, 0.0).astype(BF)
    row = iota((160, 256), 0)
    high = 8 * me + (row >> 4) - 1
    target = ((row >> 2) & 3) * 64 + (high >> 3) * 32 + (row & 3) * 8 + (high & 7)
    lift = one_hot(jnp.where((high >= 0) & (high < 16), target, -1), (160, 256))
    for s in range(2):
        for d in range(10):
            x = jnp.concatenate(
                [img[half, s, :, d].astype(F32).reshape(32, 256) for half in range(2)], axis=0
            ).astype(BF)
            y = dot(x, shifts).astype(BF)
            y = jnp.concatenate([y[:, o * 128 : o * 128 + 128] for o in range(4)], axis=0)
            t = dot(lift, y).astype(BF)
            for hh in range(10):
                for od in range(4):
                    for oh in range(4):
                        if (d - od) % 2 == 0 and (hh - oh) % 2 == 0:
                            d2, h2 = (d - od) // 2, (hh - oh) // 2
                            if 0 <= d2 < 4 and 0 <= h2 < 4:
                                r = (od * 4 + oh) * 16
                                i_buf[r : r + 16, cell(s, d2, h2)] = t[hh * 16 : hh * 16 + 16]

    taps = {}
    for a in range(3):
        for b in range(3):
            for c in range(3):
                (sd, pd_), (sh, ph), (sw, pw) = TAP[a], TAP[b], TAP[c]
                taps[(pd_, pw, ph, sd, sh, sw)] = a * 9 + b * 3 + c
    bands = []
    zero = jnp.zeros((16, 32), F32)
    for p in range(8):
        phase = (p // 4, (p // 2) % 2, p % 2)
        pieces = []
        for s in range(8):
            t = taps.get(phase + (s // 4, (s // 2) % 2, s % 2))
            pieces.append(zero if t is None else weight[t].astype(F32))
        bands.append(jnp.concatenate(pieces, axis=1))
    matrix = jnp.concatenate(bands, axis=0).astype(BF)

    deep = jnp.zeros((128, 256), F32)
    first = jnp.zeros((128, 256), F32)
    first_sum = jnp.zeros((128, 128), F32)
    step = 512
    for at in range(0, 4096, step):
        part = slice(at, at + step)
        g = g_buf[:, part]
        pre = ph_buf[:, part].astype(F32)
        grad = dot(matrix, g).astype(BF).astype(F32)
        grad = (grad * jnp.where(pre > 0, 1.0, SLOPE)).astype(BF)
        act = jnp.where(pre > 0, pre, SLOPE * pre).astype(BF)
        wide = grad.astype(F32)
        for o in range(0, step, 128):
            first_sum = first_sum + wide[:, o : o + 128]
        deep = deep + dot_nt(act, g)
        first = first + dot_nt(grad, i_buf[:, part])

    order = sorted((t, key) for key, t in taps.items())
    blocks = []
    for t, (pd_, pw, ph, sd, sh, sw) in order:
        r = (pd_ * 4 + pw * 2 + ph) * 16
        c = (sd * 4 + sh * 2 + sw) * 32
        blocks.append(deep[r : r + 16, c : c + 32])
    blocks += [zero] * 5
    for q in range(4):
        out[q * 16 : q * 16 + 16, :] = jnp.concatenate(blocks[q * 8 : q * 8 + 8], axis=1)
    total = jnp.zeros((16, 256), F32)
    bias = jnp.sum(first_sum, axis=1, keepdims=True)
    first_bias = jnp.zeros((16, 1), F32)
    for p in range(8):
        pd_, pw, ph = p // 4, (p // 2) % 2, p % 2
        move = pd_ * 64 + ph * 16 + pw * 4
        piece = first[p * 16 : p * 16 + 16]
        total = total + (pltpu.roll(piece, 256 - move, 1) if move else piece)
        first_bias = first_bias + bias[p * 16 : p * 16 + 16]
    deep_bias = jnp.sum(deep_sum, axis=1, keepdims=True)
    lane = iota((16, 256), 1)
    total = jnp.where(lane == 12, first_bias, total)
    total = jnp.where(lane == 13, deep_bias[0:16], total)
    total = jnp.where(lane == 14, deep_bias[16:32], total)
    out[64:80, :] = total
    if out.shape[0] > 80:
        out[80:, :] = jnp.zeros((out.shape[0] - 80, 256), F32)


def compute(rows, hidden, img_all, pd_all, pool_all, weight):
    return pl.pallas_call(
        compute_kernel,
        out_shape=jax.ShapeDtypeStruct((rows, 256), F32),
        in_specs=[vmem()] * 5,
        out_specs=vmem(),
        scratch_shapes=[
            pltpu.VMEM((128, 4096), BF),
            pltpu.VMEM((256, 4096), BF),
            pltpu.VMEM((256, 4096), BF),
        ],
    )(hidden, img_all, pd_all, pool_all, weight)


def reduce_kernel(members, heights, src, whole, arrived, mine, sems):
    me = lax.axis_index("depth") * heights + lax.axis_index("height")
    size = src.shape[0] // members
    barrier = pltpu.get_barrier_semaphore()

    def device(index):
        return {"depth": index // heights, "height": index % heights}

    peers = [lax.rem(me + j, members) for j in range(members)]
    for j in range(1, members):
        pl.semaphore_signal(barrier, inc=1, device_id=device(peers[j]), device_id_type=MESH)
    pl.semaphore_wait(barrier, members - 1)

    def block(index):
        return pl.ds(pl.multiple_of(index * size, 8), size)

    scatter = []
    for j in range(1, members):
        scatter.append(
            pltpu.make_async_remote_copy(
                src_ref=src.at[block(peers[j])],
                dst_ref=arrived.at[j],
                send_sem=sems.at[0, j],
                recv_sem=sems.at[1, j],
                device_id=device(peers[j]),
                device_id_type=MESH,
            )
        )
    for c in scatter:
        c.start()
    total = src[block(me), :]
    for j, c in enumerate(scatter):
        c.wait_recv()
        total = total + arrived[j + 1]
    mine[...] = total
    whole[block(me), :] = total
    gather = []
    for j in range(1, members):
        gather.append(
            pltpu.make_async_remote_copy(
                src_ref=mine,
                dst_ref=whole.at[block(me)],
                send_sem=sems.at[2, j],
                recv_sem=sems.at[3, j],
                device_id=device(peers[j]),
                device_id_type=MESH,
            )
        )
    for c in gather:
        c.start()
    for c in scatter:
        c.wait_send()
    for j in range(1, members):
        source = lax.rem(me + members - j, members)
        pltpu.make_async_remote_copy(
            src_ref=mine,
            dst_ref=whole.at[block(source)],
            send_sem=sems.at[2, j],
            recv_sem=sems.at[3, j],
            device_id=device(source),
            device_id_type=MESH,
        ).wait_recv()
    for c in gather:
        c.wait_send()


def unpack_kernel(whole, deep, first, deep_bias, first_bias):
    for t in range(27):
        r, c = (t // 8) * 16, (t % 8) * 32
        deep[t] = whole[r : r + 16, c : c + 32]
    flipped = jnp.transpose(whole[64:80, :])
    for t in range(27):
        r = (t // 9) * 64 + ((t // 3) % 3) * 16 + (t % 3) * 4
        first[t] = flipped[r : r + 4]
    first_bias[...] = flipped[12:13]
    deep_bias[...] = jnp.concatenate([flipped[13:14], flipped[14:15]], axis=1)


def reduce_all(members, heights, packed):
    size = packed.shape[0] // members
    return pl.pallas_call(
        functools.partial(reduce_kernel, members, heights),
        out_shape=jax.ShapeDtypeStruct(packed.shape, F32),
        in_specs=[vmem()],
        out_specs=vmem(),
        scratch_shapes=[
            pltpu.VMEM((members, size, 256), F32),
            pltpu.VMEM((size, 256), F32),
            pltpu.SemaphoreType.DMA((4, members)),
        ],
        compiler_params=pltpu.CompilerParams(collective_id=1, has_side_effects=True),
    )(packed)


def unpack(whole):
    return pl.pallas_call(
        unpack_kernel,
        out_shape=(
            jax.ShapeDtypeStruct((27, 16, 32), F32),
            jax.ShapeDtypeStruct((27, 4, 16), F32),
            jax.ShapeDtypeStruct((1, 32), F32),
            jax.ShapeDtypeStruct((1, 16), F32),
        ),
        in_specs=[vmem()],
        out_specs=(vmem(),) * 4,
    )(whole)


def on_device(count, heights, images, pre_hidden, pre_deep, pooled_grad, deep_weight):
    img_all, pd_all, pool_all = exchange(count, images, pre_deep[0], pooled_grad[0])
    weight = deep_weight.transpose(2, 3, 4, 1, 0).reshape(27, 16, 32)
    members = count * heights
    size = 8 * (-(-80 // (8 * members)))
    packed = compute(members * size, pre_hidden, img_all, pd_all, pool_all, weight)
    deep, first, deep_bias, first_bias = unpack(reduce_all(members, heights, packed))
    return (
        first.reshape(3, 3, 3, 4, 16).transpose(4, 3, 0, 1, 2),
        first_bias.reshape(16),
        deep.reshape(3, 3, 3, 16, 32).transpose(4, 3, 0, 1, 2),
        deep_bias.reshape(32),
    )


def solution(mesh):
    return jax.shard_map(
        functools.partial(on_device, mesh.shape["depth"], mesh.shape["height"]),
        mesh=mesh,
        in_specs=(
            P("groups", None, "depth", "height", None),
            P("groups", None, "depth", "height", None),
            P(("groups", "height"), None, "depth", None, None),
            P(("groups", "height"), None, "depth", None),
            P(),
        ),
        out_specs=(
            P("groups", None, None, None, None),
            P("groups"),
            P("groups", None, None, None, None),
            P("groups"),
        ),
        check_vma=False,
    )
```

time: 233 us -> 40.5 us (0.17)
  local copies, waits for them, and re-layouts: 95.9 us -> 0 us
  blocking collectives: 74.3 us -> 0 us
  Pallas kernels: 0 us -> 39.7 us
  matrix products: 37.7 us -> 0 us
  starting transfers between devices: 16.9 us -> 0 us
  other arithmetic: 4.49 us -> 0 us
    psum x1 -> x0, blocking collectives: 63.7 us -> none  [on_device(): lax.psum((first_kernel, first_bias, deep_kernel, deep_bias), ('depth', 'h...]
    reshape x2 -> x0, local copies, waits for them, and re-layouts: 46.6 us -> none  [deep_weight_grad(): grown.reshape(samples, chans, coarse_depth + 1, 2, coarse_height + 1, 2,...]
    pallas_call x0 -> x4, Pallas kernels: none -> 39.7 us  [the longest x1 15.6 us: reduce_all(): pl.pallas_call(functools.partial(reduce_kernel, members, heights), out_sh...]
    dot_general x62 -> x0, matrix products: 37.7 us -> none  [the longest x27 29 us: first_weight_grad(): jnp.einsum('sodhw,sidhw->oi', first_grad, view, preferred_element_type=jn...]
    convert_element_type x3 -> x0, local copies, waits for them, and re-layouts: 21.3 us -> none  [the longest x2 21.2 us: transpose_conv(): return woven.astype(jnp.bfloat16)]
    ppermute x6 -> x0, starting transfers between devices: 16.9 us -> none  [the longest x2 8.18 us: padded_2(): lax.ppermute(lax.slice_in_dim(block, block.shape[dim] - width, None, axis...]
    pad x1 -> x0, local copies, waits for them, and re-layouts: 10.9 us -> none  [deep_weight_grad(): grown = jnp.pad(padded, ((0, 0), (0, 0), (0, 1), (0, 1), (0, 1)))]
    all_to_all x2 -> x0, blocking collectives: 10.6 us -> none  [the longest x1 5.92 us: on_device(): lax.all_to_all(returned, 'height', split_axis=3, concat_axis=0, tiled=True)]
  transfers between devices with their start and end apart: 6 -> 0, of which waited for: 0 -> 0; matrix products, arithmetic and copies ran while one was open for 29% -> 0% of each run, Pallas kernels for 0% -> 0%
where the time goes in v1:
time: 40.5 us; the launch traced here: 40.3 us
  Pallas kernels  39.7 us (98%)
  between operations  0.65 us (2%)
    pallas_call x1, Pallas kernels, reduce_all(): pl.pallas_call(functools.partial(reduce_kernel, members, heights), out_sh...  15.6 us
    pallas_call x1, Pallas kernels, exchange(): pl.pallas_call(functools.partial(exchange_kernel, count), out_shape=(jax....  12.9 us
    pallas_call x1, Pallas kernels, compute(): pl.pallas_call(compute_kernel, out_shape=jax.ShapeDtypeStruct((rows, 256)...  9.36 us
    pallas_call x1, Pallas kernels, unpack(): pl.pallas_call(unpack_kernel, out_shape=(jax.ShapeDtypeStruct((27, 16, 32...  1.76 us

profile of v1, /device:TPU:0, one launch (start us, length us, event | category | flops | bytes accessed | tf_op | source)
XLA Modules:
  0.0 40.3 jit_solution(14284792093401998760)
XLA Ops:
  0.6 12.9 %shard_map.84 = (bf16[2,2,4,10,8,256]{5,4,3,2,1,0:T(8,128)(2,1)}, bf16[2,32,5,8,128]{4,3,2,1,0:T(8,128)(2,1)}, bf16[2,2,32,2,256]{4,3,2,1,0:T(2,128)(2,1)}) custom-call(bf16[2,4,8,8,256]{4,3,2,1,0:T(8,128)(2,1)} %img.1, bf16[32,4,8,128]{3,2,1,0:T(8,128)(2,1)} %bitcast.13, bf16[32,2,256]{2,1,0:T(2,128)(2,1)} %bitcast.15), custom_call_target="tpu_custom_call" | custom-call | tf_op jit(solution)/shard_map/pallas_call | solution.py:147
  13.6 9.4 %shard_map.85.src = f32[128,256]{1,0:T(8,128)} custom-call(bf16[2,16,8,8,256]{4,3,2,1,0:T(8,128)(2,1)} %hid.1, bf16[2,2,4,10,8,256]{5,4,3,2,1,0:T(8,128)(2,1)} %get-tuple-element.11.img, bf16[2,32,5,8,128]{4,3,2,1,0:T(8,128)(2,1)} %get-tuple-element.12.pd, bf16[2,2,32,2,256]{4,3,2,1,0:T(2,128)(2,1)} %get-tuple-element.13.pool, bf16[27,16,32]{2,1,0:T(8,128)(2,1)} %bitcast.14), custom_call_target="tpu_custom_call" | custom-call | tf_op jit(solution)/shard_map/pallas_call | solution.py:304
  22.9 15.6 %shard_map.86.whole = f32[128,256]{1,0:T(8,128)} custom-call(f32[128,256]{1,0:T(8,128)} %shard_map.85.src), custom_call_target="tpu_custom_call" | custom-call | tf_op jit(solution)/shard_map/pallas_call | solution.py:397
  38.6 1.8 %shard_map.87 = (f32[27,16,32]{2,1,0:T(8,128)}, f32[27,4,16]{2,1,0:T(4,128)}, f32[1,32]{1,0:T(1,128)}, f32[1,16]{1,0:T(1,128)}) custom-call(f32[128,256]{1,0:T(8,128)} %shard_map.86.whole), custom_call_target="tpu_custom_call" | custom-call | tf_op jit(solution)/shard_map/pallas_call | solution.py:412

commit v2 on v1

v2 whole, which is shorter than its diff:
```python
import functools

import jax
import jax.numpy as jnp
from jax import lax
from jax.experimental import pallas as pl
from jax.experimental.pallas import tpu as pltpu
from jax.sharding import PartitionSpec as P

SLOPE = 0.3
MESH = pl.DeviceIdType.MESH
BF = jnp.bfloat16
F32 = jnp.float32
TAP = ((1, 1), (0, 0), (0, 1))


def vmem():
    return pl.BlockSpec(memory_space=pltpu.VMEM)


def iota(shape, dim):
    return lax.broadcasted_iota(jnp.int32, shape, dim)


def one_hot(row_target, shape):
    return jnp.where(row_target == iota(shape, 1), 1.0, 0.0).astype(BF)


def dot(a, b):
    return jnp.dot(a, b, preferred_element_type=F32)


def dot_nt(a, b):
    return lax.dot_general(a, b, (((1,), (1,)), ((), ())), preferred_element_type=F32)


def fused_kernel(
    count, heights, hid, img, pd, pool, weight, whole,
    img_all, pd_all, pool_all, ph_buf, g_buf, i_buf, src, arrived, mine, send, recv, sems,
):
    k = lax.axis_index("depth")
    h = lax.axis_index("height")
    members = count * heights
    index = k * heights + h
    cells = img.shape[2]
    quarter = pd.shape[1]

    def device(number):
        return {"depth": number // heights, "height": number % heights}

    peers = [lax.rem(index + j, members) for j in range(members)]
    barrier = pltpu.get_barrier_semaphore()
    for j in range(1, members):
        pl.semaphore_signal(barrier, inc=1, device_id=device(peers[j]), device_id_type=MESH)

    def cell(s, d2, h2):
        at = ((s * 4 + d2) * 4 + h2) * 128
        return slice(at, at + 128)

    row = iota((128, 128), 0)
    order = one_hot((row & 15) * 8 + (row >> 4), (128, 128))
    z = iota((256, 256), 0)
    col = iota((256, 256), 1)
    split = jnp.where(z == 2 * (col & 127) + (col >> 7), 1.0, 0.0).astype(BF)

    def hidden_rows(s, d):
        x = hid[s, :, d].astype(F32).reshape(128, 256).astype(BF)
        a = dot(x, split).astype(BF)
        b = dot(order, a).astype(BF)
        for h2 in range(4):
            for pw in range(2):
                r = (d % 2) * 64 + pw * 32
                ph_buf[r : r + 32, cell(s, d // 2, h2)] = b[
                    h2 * 32 : h2 * 32 + 32, pw * 128 : pw * 128 + 128
                ]

    for s in range(2):
        for d in range(8):
            hidden_rows(s, d)

    pl.semaphore_wait(barrier, members - 1)

    def copy(src_ref, dst_ref, slot, depth, height):
        return pltpu.make_async_remote_copy(
            src_ref=src_ref,
            dst_ref=dst_ref,
            send_sem=send.at[slot],
            recv_sem=recv.at[slot],
            device_id={"depth": depth, "height": height},
            device_id_type=MESH,
        )

    def partner(slot):
        return [
            copy(pd, pd_all.at[slot, :, 0:quarter], 0, k, 1 - h),
            copy(pool, pool_all.at[slot, 0], 1, k, 1 - h),
            copy(img, img_all.at[slot, :, :, 1 : cells + 1], 2, k, 1 - h),
        ]

    def down():
        return [
            copy(pd.at[:, 0:1], pd_all.at[h, :, quarter : quarter + 1], 3, k - 1, h),
            copy(pool, pool_all.at[h, 1], 4, k - 1, h),
            copy(img.at[:, :, 0:1], img_all.at[h, :, :, cells + 1 : cells + 2], 5, k - 1, h),
        ]

    def up():
        return [copy(img.at[:, :, cells - 1 : cells], img_all.at[h, :, :, 0:1], 6, k + 1, h)]

    def relay_above(slot):
        parts = [
            pd_all.at[slot, :, quarter : quarter + 1],
            pool_all.at[slot, 1],
            img_all.at[slot, :, :, cells + 1 : cells + 2],
        ]
        return [copy(p, p, 7 + n, k, 1 - h) for n, p in enumerate(parts)]

    def relay_below(slot):
        part = img_all.at[slot, :, :, 0:1]
        return [copy(part, part, 10, k, 1 - h)]

    @pl.when(k > 0)
    def _():
        for c in down():
            c.start()

    @pl.when(k < count - 1)
    def _():
        for c in up():
            c.start()

    for c in partner(h):
        c.start()
    img_all[h, :, :, 1 : cells + 1] = img[...]
    pd_all[h, :, 0:quarter] = pd[...]
    pool_all[h, 0] = pool[...]

    @pl.when(k == 0)
    def _():
        img_all[:, :, :, 0:1] = jnp.zeros_like(img_all[:, :, :, 0:1])

    @pl.when(k == count - 1)
    def _():
        img_all[:, :, :, cells + 1 : cells + 2] = jnp.zeros_like(img_all[:, :, :, 0:1])
        pd_all[:, :, quarter : quarter + 1] = jnp.zeros_like(pd_all[:, :, 0:1])
        pool_all[:, 1] = jnp.zeros_like(pool_all[:, 1])

    taps = {}
    for a in range(3):
        for b in range(3):
            for c in range(3):
                (sd, pd_), (sh, ph), (sw, pw) = TAP[a], TAP[b], TAP[c]
                taps[(pd_, pw, ph, sd, sh, sw)] = a * 9 + b * 3 + c
    bands = []
    zero = jnp.zeros((16, 32), F32)
    for p in range(8):
        phase = (p // 4, (p // 2) % 2, p % 2)
        pieces = []
        for s in range(8):
            t = taps.get(phase + (s // 4, (s // 2) % 2, s % 2))
            pieces.append(zero if t is None else weight[t].astype(F32))
        bands.append(jnp.concatenate(pieces, axis=1))
    matrix = jnp.concatenate(bands, axis=0).astype(BF)

    row = iota((160, 256), 0)
    high = 4 * h + (row >> 5)
    pick = one_hot(jnp.where(high < 8, (row & 31) * 8 + high, -1), (160, 256))
    r640 = iota((256, 640), 0)
    c640 = iota((256, 640), 1)
    spread_mat = jnp.where(
        r640 == ((4 * h + (c640 >> 7)) >> 1) * 64 + ((c640 & 127) >> 1), 1.0, 0.0
    ).astype(BF)
    z = iota((256, 512), 0)
    col = iota((256, 512), 1)
    shifts = jnp.where(z == 2 * (col & 127) + (col >> 7) - 1, 1.0, 0.0).astype(BF)
    high = 8 * h + (row >> 4) - 1
    target = ((row >> 2) & 3) * 64 + (high >> 3) * 32 + (row & 3) * 8 + (high & 7)
    lift = one_hot(jnp.where((high >= 0) & (high < 16), target, -1), (160, 256))
    lane = iota((32, 128), 1)

    for c in partner(1 - h):
        c.wait_recv()

    sums = {"deep": jnp.zeros((32, 128), F32)}

    def gradient_rows(s, depths):
        coarse = pool_all[s, depths[0] // 4].astype(F32)
        spread = dot(coarse[:, (depths[0] // 2) % 2, :].astype(BF), spread_mat) / 8.0
        for d in depths:
            x = pd_all[s, :, d].astype(F32).reshape(256, 128).astype(BF)
            y = dot(pick, x)
            for j in range(5):
                slope = jnp.where(y[j * 32 : j * 32 + 32] > 0, 1.0, SLOPE)
                g = (spread[:, j * 128 : j * 128 + 128] * slope).astype(BF)
                wide = g.astype(F32)
                if d < 4 and j < 4:
                    sums["deep"] = sums["deep"] + wide
                moved = jnp.where(lane < 127, pltpu.roll(wide, 127, 1), 0.0).astype(BF)
                for sd in range(2):
                    for sh in range(2):
                        if 0 <= d - sd < 4 and 0 <= j - sh < 4:
                            at = cell(s, d - sd, j - sh)
                            r = (sd * 4 + sh * 2) * 32
                            g_buf[r : r + 32, at] = g
                            g_buf[r + 32 : r + 64, at] = moved

    def image_rows(s, d):
        x = jnp.concatenate(
            [img_all[half, s, :, d].astype(F32).reshape(32, 256) for half in range(2)], axis=0
        ).astype(BF)
        y = dot(x, shifts).astype(BF)
        y = jnp.concatenate([y[:, o * 128 : o * 128 + 128] for o in range(4)], axis=0)
        t = dot(lift, y).astype(BF)
        for hh in range(10):
            for od in range(4):
                for oh in range(4):
                    if (d - od) % 2 == 0 and (hh - oh) % 2 == 0:
                        d2, h2 = (d - od) // 2, (hh - oh) // 2
                        if 0 <= d2 < 4 and 0 <= h2 < 4:
                            r = (od * 4 + oh) * 16
                            i_buf[r : r + 16, cell(s, d2, h2)] = t[hh * 16 : hh * 16 + 16]

    sums["kernel"] = jnp.zeros((128, 256), F32)
    sums["first"] = jnp.zeros((128, 256), F32)
    sums["bias"] = jnp.zeros((128, 128), F32)

    def contract(s, d2):
        at = (s * 4 + d2) * 512
        part = slice(at, at + 512)
        g = g_buf[:, part]
        pre = ph_buf[:, part].astype(F32)
        grad = dot(matrix, g).astype(BF).astype(F32)
        grad = (grad * jnp.where(pre > 0, 1.0, SLOPE)).astype(BF)
        act = jnp.where(pre > 0, pre, SLOPE * pre).astype(BF)
        wide = grad.astype(F32)
        for o in range(0, 512, 128):
            sums["bias"] = sums["bias"] + wide[:, o : o + 128]
        sums["kernel"] = sums["kernel"] + dot_nt(act, g)
        sums["first"] = sums["first"] + dot_nt(grad, i_buf[:, part])

    for s in range(2):
        gradient_rows(s, (0, 1))
        gradient_rows(s, (2, 3))
        for d in range(1, 9):
            image_rows(s, d)

    @pl.when(k < count - 1)
    def _():
        for c, r in zip(down(), relay_above(h)):
            c.wait_recv()
            r.start()

    @pl.when(k > 0)
    def _():
        for c, r in zip(up(), relay_below(h)):
            c.wait_recv()
            r.start()

    for s in range(2):
        contract(s, 1)
        contract(s, 2)

    @pl.when(k < count - 1)
    def _():
        for c in relay_above(1 - h):
            c.wait_recv()

    @pl.when(k > 0)
    def _():
        for c in relay_below(1 - h):
            c.wait_recv()

    for s in range(2):
        gradient_rows(s, (4,))
        image_rows(s, 0)
        image_rows(s, 9)
        contract(s, 0)
        contract(s, 3)

    deep, first = sums["kernel"], sums["first"]
    blocks = []
    for t, (pd_, pw, ph, sd, sh, sw) in sorted((t, key) for key, t in taps.items()):
        r = (pd_ * 4 + pw * 2 + ph) * 16
        c = (sd * 4 + sh * 2 + sw) * 32
        blocks.append(deep[r : r + 16, c : c + 32])
    total = jnp.zeros((16, 256), F32)
    bias = jnp.sum(sums["bias"], axis=1, keepdims=True)
    first_bias = jnp.zeros((16, 1), F32)
    for p in range(8):
        pd_, pw, ph = p // 4, (p // 2) % 2, p % 2
        move = pd_ * 64 + ph * 16 + pw * 4
        piece = first[p * 16 : p * 16 + 16]
        total = total + (pltpu.roll(piece, 256 - move, 1) if move else piece)
        first_bias = first_bias + bias[p * 16 : p * 16 + 16]
    deep_bias = jnp.sum(sums["deep"], axis=1, keepdims=True)
    lane = iota((16, 256), 1)
    total = jnp.where(lane == 12, first_bias, total)
    total = jnp.where(lane == 13, deep_bias[0:16], total)
    total = jnp.where(lane == 14, deep_bias[16:32], total)
    blocks.append(jnp.concatenate([total[:, 160:176], jnp.zeros((16, 16), F32)], axis=1))
    for q in range(7):
        src[q * 16 : q * 16 + 16, :] = jnp.concatenate(blocks[q * 4 : q * 4 + 4], axis=1)
    src[112:128, :] = jnp.concatenate([total[:, 0:48], total[:, 64:112], total[:, 128:160]], axis=1)
    if src.shape[0] > 128:
        src[128:, :] = jnp.zeros((src.shape[0] - 128, 128), F32)

    size = src.shape[0] // members

    def block(number):
        return pl.ds(pl.multiple_of(number * size, 8), size)

    def hop(src_ref, dst_ref, phase, j, number):
        return pltpu.make_async_remote_copy(
            src_ref=src_ref,
            dst_ref=dst_ref,
            send_sem=sems.at[2 * phase, j],
            recv_sem=sems.at[2 * phase + 1, j],
            device_id=device(number),
            device_id_type=MESH,
        )

    scatter = [hop(src.at[block(peers[j])], arrived.at[j], 0, j, peers[j]) for j in range(1, members)]
    for c in scatter:
        c.start()
    total = src[block(index), :]
    for j, c in enumerate(scatter):
        c.wait_recv()
        total = total + arrived[j + 1]
    mine[...] = total
    whole[block(index), :] = total
    gather = [hop(mine, whole.at[block(index)], 1, j, peers[j]) for j in range(1, members)]
    for c in gather:
        c.start()

    for c in scatter + partner(h):
        c.wait_send()

    @pl.when(k > 0)
    def _():
        for c in down() + relay_below(h):
            c.wait_send()

    @pl.when(k < count - 1)
    def _():
        for c in up() + relay_above(h):
            c.wait_send()

    for j in range(1, members):
        source = lax.rem(index + members - j, members)
        hop(mine, whole.at[block(source)], 1, j, source).wait_recv()
    for c in gather:
        c.wait_send()


def fused(count, heights, hidden, images, pre_deep, pooled, weight):
    samples, chans, cells, rows, width = images.shape
    out_chans, coarse, coarse_rows, coarse_width = pre_deep.shape
    members = count * heights
    size = 8 * (-(-128 // (8 * members)))
    return pl.pallas_call(
        functools.partial(fused_kernel, count, heights),
        out_shape=jax.ShapeDtypeStruct((members * size, 128), F32),
        in_specs=[vmem()] * 5,
        out_specs=vmem(),
        scratch_shapes=[
            pltpu.VMEM((2, samples, chans, cells + 2, rows, width), BF),
            pltpu.VMEM((2, out_chans, coarse + 1, coarse_rows, coarse_width), BF),
            pltpu.VMEM((2, 2) + pooled.shape, BF),
            pltpu.VMEM((128, 4096), BF),
            pltpu.VMEM((256, 4096), BF),
            pltpu.VMEM((256, 4096), BF),
            pltpu.VMEM((members * size, 128), F32),
            pltpu.VMEM((members, size, 128), F32),
            pltpu.VMEM((size, 128), F32),
            pltpu.SemaphoreType.DMA((11,)),
            pltpu.SemaphoreType.DMA((11,)),
            pltpu.SemaphoreType.DMA((4, members)),
        ],
        compiler_params=pltpu.CompilerParams(collective_id=0, has_side_effects=True),
    )(hidden, images, pre_deep, pooled, weight)


def unpack_kernel(whole, deep, first, deep_bias, first_bias):
    for t in range(27):
        r, c = (t // 4) * 16, (t % 4) * 32
        deep[t] = whole[r : r + 16, c : c + 32]
    flipped = jnp.transpose(whole[112:128, :])
    rest = jnp.transpose(whole[96:112, :])[96:112]
    for t in range(27):
        r = (t // 9) * 48 + ((t // 3) % 3) * 16 + (t % 3) * 4
        first[t] = flipped[r : r + 4] if r < 128 else rest[r - 128 : r - 124]
    first_bias[...] = flipped[12:13]
    deep_bias[...] = jnp.concatenate([flipped[13:14], flipped[14:15]], axis=1)


def unpack(whole):
    return pl.pallas_call(
        unpack_kernel,
        out_shape=(
            jax.ShapeDtypeStruct((27, 16, 32), F32),
            jax.ShapeDtypeStruct((27, 4, 16), F32),
            jax.ShapeDtypeStruct((1, 32), F32),
            jax.ShapeDtypeStruct((1, 16), F32),
        ),
        in_specs=[vmem()],
        out_specs=(vmem(),) * 4,
    )(whole)


def on_device(count, heights, images, pre_hidden, pre_deep, pooled_grad, deep_weight):
    weight = deep_weight.transpose(2, 3, 4, 1, 0).reshape(27, 16, 32)
    whole = fused(count, heights, pre_hidden, images, pre_deep[0], pooled_grad[0], weight)
    deep, first, deep_bias, first_bias = unpack(whole)
    return (
        first.reshape(3, 3, 3, 4, 16).transpose(4, 3, 0, 1, 2),
        first_bias.reshape(16),
        deep.reshape(3, 3, 3, 16, 32).transpose(4, 3, 0, 1, 2),
        deep_bias.reshape(32),
    )


def solution(mesh):
    return jax.shard_map(
        functools.partial(on_device, mesh.shape["depth"], mesh.shape["height"]),
        mesh=mesh,
        in_specs=(
            P("groups", None, "depth", "height", None),
            P("groups", None, "depth", "height", None),
            P(("groups", "height"), None, "depth", None, None),
            P(("groups", "height"), None, "depth", None),
            P(),
        ),
        out_specs=(
            P("groups", None, None, None, None),
            P("groups"),
            P("groups", None, None, None, None),
            P("groups"),
        ),
        check_vma=False,
    )
```

time: 40.5 us -> 28.1 us (0.69)
  Pallas kernels: 39.7 us -> 27.2 us
    pallas_call x3 -> x1, Pallas kernels: 37.9 us -> 25.5 us  [fused(): pl.pallas_call(functools.partial(fused_kernel, count, heights), out_shape...]
where the time goes in v2:
time: 28.1 us; the launch traced here: 27.9 us
  Pallas kernels  27.2 us (97%)
  between operations  0.64 us (2%)
    pallas_call x1, Pallas kernels, fused(): pl.pallas_call(functools.partial(fused_kernel, count, heights), out_shape...  25.5 us
    pallas_call x1, Pallas kernels, unpack(): pl.pallas_call(unpack_kernel, out_shape=(jax.ShapeDtypeStruct((27, 16, 32...  1.73 us

profile of v2, /device:TPU:0, one launch (start us, length us, event | category | flops | bytes accessed | tf_op | source)
XLA Modules:
  0.0 27.9 jit_solution(8136678693291960979)
XLA Ops:
  0.6 25.5 %shard_map.84.whole = f32[128,128]{1,0:T(8,128)} custom-call(bf16[2,16,8,8,256]{4,3,2,1,0:T(8,128)(2,1)} %hid.1, bf16[2,4,8,8,256]{4,3,2,1,0:T(8,128)(2,1)} %img.1, bf16[32,4,8,128]{3,2,1,0:T(8,128)(2,1)} %bitcast.13, bf16[32,2,256]{2,1,0:T(2,128)(2,1)} %bitcast.15, bf16[27,16,32]{2,1,0:T(8,128)(2,1)} %bitcast.14), custom_call_target="tpu_custom_call" | custom-call | tf_op jit(solution)/shard_map/pallas_call | solution.py:360
  26.1 1.7 %shard_map.85 = (f32[27,16,32]{2,1,0:T(8,128)}, f32[27,4,16]{2,1,0:T(4,128)}, f32[1,32]{1,0:T(1,128)}, f32[1,16]{1,0:T(1,128)}) custom-call(f32[128,128]{1,0:T(8,128)} %shard_map.84.whole), custom_call_target="tpu_custom_call" | custom-call | tf_op jit(solution)/shard_map/pallas_call | solution.py:397

commit v3 on v2

--- a/solution.py
+++ b/solution.py
@@ -35,27 +35,50 @@
 
 
 def fused_kernel(
-    count, heights, hid, img, pd, pool, weight, whole,
-    img_all, pd_all, pool_all, ph_buf, g_buf, i_buf, src, arrived, mine, send, recv, sems,
+    count, heights, hid_in, img_in, pd_in, pool_in, weight_in, whole,
+    hid, weight, img_all, pd_all, pool_all, ph_buf, f_buf, g_buf, y_buf, i_buf, src, arrived, mine,
+    local, send, recv, sems,
 ):
     k = lax.axis_index("depth")
     h = lax.axis_index("height")
     members = count * heights
     index = k * heights + h
-    cells = img.shape[2]
-    quarter = pd.shape[1]
+    cells = img_in.shape[2]
+    quarter = pd_in.shape[1]
 
     def device(number):
         return {"depth": number // heights, "height": number % heights}
 
-    peers = [lax.rem(index + j, members) for j in range(members)]
+    def flipped(j):
+        if members & (members - 1):
+            return lax.rem(index + j, members)
+        total, bit = 0, 1
+        while bit < members:
+            digit = (index // bit) % 2
+            total = total + bit * (1 - digit if j & bit else digit)
+            bit *= 2
+        return total
+
+    def origin(j):
+        if members & (members - 1):
+            return lax.rem(index + members - j, members)
+        return flipped(j)
+
+    turns = list(range(members - 1, 0, -1))
+    peers = {j: flipped(j) for j in turns}
     barrier = pltpu.get_barrier_semaphore()
-    for j in range(1, members):
+    for j in turns:
         pl.semaphore_signal(barrier, inc=1, device_id=device(peers[j]), device_id_type=MESH)
 
-    def cell(s, d2, h2):
-        at = ((s * 4 + d2) * 4 + h2) * 128
-        return slice(at, at + 128)
+    loads = [
+        pltpu.make_async_copy(hid_in, hid, local.at[0]),
+        pltpu.make_async_copy(pd_in, pd_all.at[h, :, 0:quarter], local.at[1]),
+        pltpu.make_async_copy(pool_in, pool_all.at[h, 0], local.at[2]),
+        pltpu.make_async_copy(img_in, img_all.at[h, :, :, 1 : cells + 1], local.at[3]),
+        pltpu.make_async_copy(weight_in, weight, local.at[4]),
+    ]
+    for c in loads:
+        c.start()
 
     row = iota((128, 128), 0)
     order = one_hot((row & 15) * 8 + (row >> 4), (128, 128))
@@ -70,13 +93,33 @@
         for h2 in range(4):
             for pw in range(2):
                 r = (d % 2) * 64 + pw * 32
-                ph_buf[r : r + 32, cell(s, d // 2, h2)] = b[
+                at = (d // 2) * 1024 + s * 512 + h2 * 128
+                ph_buf[r : r + 32, at : at + 128] = b[
                     h2 * 32 : h2 * 32 + 32, pw * 128 : pw * 128 + 128
                 ]
 
+    loads[0].wait()
     for s in range(2):
         for d in range(8):
             hidden_rows(s, d)
+
+    row = iota((160, 256), 0)
+    high = 4 * h + (row >> 5)
+    pick = one_hot(jnp.where(high < 8, (row & 31) * 8 + high, -1), (160, 256))
+    r640 = iota((256, 640), 0)
+    c640 = iota((256, 640), 1)
+    spread_mat = jnp.where(
+        r640 == ((4 * h + (c640 >> 7)) >> 1) * 64 + ((c640 & 127) >> 1), 1.0, 0.0
+    ).astype(BF)
+    z = iota((256, 512), 0)
+    col = iota((256, 512), 1)
+    shifts = jnp.where(z == 2 * (col & 127) + (col >> 7) - 1, 1.0, 0.0).astype(BF)
+    high = 8 * h + (row >> 4) - 1
+    target = ((row >> 2) & 3) * 64 + (high >> 3) * 32 + (row & 3) * 8 + (high & 7)
+    lift = one_hot(jnp.where((high >= 0) & (high < 16), target, -1), (160, 256))
+    lane = iota((32, 128), 1)
+    for c in loads[1:]:
+        c.wait()
 
     pl.semaphore_wait(barrier, members - 1)
 
@@ -90,34 +133,35 @@
             device_id_type=MESH,
         )
 
+    def same(part, slot):
+        return copy(part, part, slot, k, 1 - h)
+
     def partner(slot):
         return [
-            copy(pd, pd_all.at[slot, :, 0:quarter], 0, k, 1 - h),
-            copy(pool, pool_all.at[slot, 0], 1, k, 1 - h),
-            copy(img, img_all.at[slot, :, :, 1 : cells + 1], 2, k, 1 - h),
+            same(pd_all.at[slot, :, 0:quarter], 0),
+            same(pool_all.at[slot, 0], 1),
+            same(img_all.at[slot, :, :, 1 : cells + 1], 2),
         ]
 
     def down():
         return [
-            copy(pd.at[:, 0:1], pd_all.at[h, :, quarter : quarter + 1], 3, k - 1, h),
-            copy(pool, pool_all.at[h, 1], 4, k - 1, h),
-            copy(img.at[:, :, 0:1], img_all.at[h, :, :, cells + 1 : cells + 2], 5, k - 1, h),
+            copy(pd_all.at[h, :, 0:1], pd_all.at[h, :, quarter : quarter + 1], 3, k - 1, h),
+            copy(pool_all.at[h, 0], pool_all.at[h, 1], 4, k - 1, h),
+            copy(img_all.at[h, :, :, 1:2], img_all.at[h, :, :, cells + 1 : cells + 2], 5, k - 1, h),
         ]
 
     def up():
-        return [copy(img.at[:, :, cells - 1 : cells], img_all.at[h, :, :, 0:1], 6, k + 1, h)]
+        return [copy(img_all.at[h, :, :, cells : cells + 1], img_all.at[h, :, :, 0:1], 6, k + 1, h)]
 
     def relay_above(slot):
-        parts = [
-            pd_all.at[slot, :, quarter : quarter + 1],
-            pool_all.at[slot, 1],
-            img_all.at[slot, :, :, cells + 1 : cells + 2],
+        return [
+            same(pd_all.at[slot, :, quarter : quarter + 1], 7),
+            same(pool_all.at[slot, 1], 8),
+            same(img_all.at[slot, :, :, cells + 1 : cells + 2], 9),
         ]
-        return [copy(p, p, 7 + n, k, 1 - h) for n, p in enumerate(parts)]
 
     def relay_below(slot):
-        part = img_all.at[slot, :, :, 0:1]
-        return [copy(part, part, 10, k, 1 - h)]
+        return [same(img_all.at[slot, :, :, 0:1], 10)]
 
     @pl.when(k > 0)
     def _():
@@ -131,9 +175,6 @@
 
     for c in partner(h):
         c.start()
-    img_all[h, :, :, 1 : cells + 1] = img[...]
-    pd_all[h, :, 0:quarter] = pd[...]
-    pool_all[h, 0] = pool[...]
 
     @pl.when(k == 0)
     def _():
@@ -162,36 +203,23 @@
         bands.append(jnp.concatenate(pieces, axis=1))
     matrix = jnp.concatenate(bands, axis=0).astype(BF)
 
-    row = iota((160, 256), 0)
-    high = 4 * h + (row >> 5)
-    pick = one_hot(jnp.where(high < 8, (row & 31) * 8 + high, -1), (160, 256))
-    r640 = iota((256, 640), 0)
-    c640 = iota((256, 640), 1)
-    spread_mat = jnp.where(
-        r640 == ((4 * h + (c640 >> 7)) >> 1) * 64 + ((c640 & 127) >> 1), 1.0, 0.0
-    ).astype(BF)
-    z = iota((256, 512), 0)
-    col = iota((256, 512), 1)
-    shifts = jnp.where(z == 2 * (col & 127) + (col >> 7) - 1, 1.0, 0.0).astype(BF)
-    high = 8 * h + (row >> 4) - 1
-    target = ((row >> 2) & 3) * 64 + (high >> 3) * 32 + (row & 3) * 8 + (high & 7)
-    lift = one_hot(jnp.where((high >= 0) & (high < 16), target, -1), (160, 256))
-    lane = iota((32, 128), 1)
-
-    for c in partner(1 - h):
-        c.wait_recv()
-
     sums = {"deep": jnp.zeros((32, 128), F32)}
 
     def gradient_rows(s, depths):
+        x = jnp.concatenate(
+            [pd_all[s, :, d].astype(F32).reshape(256, 128).astype(BF) for d in depths], axis=1
+        )
+        y = dot(pick, x)
         coarse = pool_all[s, depths[0] // 4].astype(F32)
-        spread = dot(coarse[:, (depths[0] // 2) % 2, :].astype(BF), spread_mat) / 8.0
-        for d in depths:
-            x = pd_all[s, :, d].astype(F32).reshape(256, 128).astype(BF)
-            y = dot(pick, x)
+        halves = sorted({(d // 2) % 2 for d in depths})
+        rows = jnp.concatenate([coarse[:, n, :] for n in halves], axis=0).astype(BF)
+        spread = dot(rows, spread_mat) / 8.0
+        for n, d in enumerate(depths):
+            r = halves.index((d // 2) % 2) * 32
             for j in range(5):
-                slope = jnp.where(y[j * 32 : j * 32 + 32] > 0, 1.0, SLOPE)
-                g = (spread[:, j * 128 : j * 128 + 128] * slope).astype(BF)
+                pre = y[j * 32 : j * 32 + 32, n * 128 : n * 128 + 128]
+                slope = jnp.where(pre > 0, 1.0, SLOPE)
+                g = (spread[r : r + 32, j * 128 : j * 128 + 128] * slope).astype(BF)
                 wide = g.astype(F32)
                 if d < 4 and j < 4:
                     sums["deep"] = sums["deep"] + wide
@@ -199,50 +227,69 @@
                 for sd in range(2):
                     for sh in range(2):
                         if 0 <= d - sd < 4 and 0 <= j - sh < 4:
-                            at = cell(s, d - sd, j - sh)
-                            r = (sd * 4 + sh * 2) * 32
-                            g_buf[r : r + 32, at] = g
-                            g_buf[r + 32 : r + 64, at] = moved
-
-    def image_rows(s, d):
+                            at = pl.multiple_of((d - sd) * 1024 + s * 512 + (j - sh) * 128, 128)
+                            r2 = (sd * 4 + sh * 2) * 32
+                            g_buf[r2 : r2 + 32, pl.ds(at, 128)] = g
+                            g_buf[r2 + 32 : r2 + 64, pl.ds(at, 128)] = moved
+
+    def image_shift(half, depths):
         x = jnp.concatenate(
-            [img_all[half, s, :, d].astype(F32).reshape(32, 256) for half in range(2)], axis=0
+            [img_all[half, s, :, d].astype(F32).reshape(32, 256) for d in depths for s in range(2)], axis=0
         ).astype(BF)
         y = dot(x, shifts).astype(BF)
-        y = jnp.concatenate([y[:, o * 128 : o * 128 + 128] for o in range(4)], axis=0)
-        t = dot(lift, y).astype(BF)
-        for hh in range(10):
-            for od in range(4):
-                for oh in range(4):
-                    if (d - od) % 2 == 0 and (hh - oh) % 2 == 0:
-                        d2, h2 = (d - od) // 2, (hh - oh) // 2
-                        if 0 <= d2 < 4 and 0 <= h2 < 4:
-                            r = (od * 4 + oh) * 16
-                            i_buf[r : r + 16, cell(s, d2, h2)] = t[hh * 16 : hh * 16 + 16]
+        for n, d in enumerate(depths):
+            for s in range(2):
+                r = (n * 2 + s) * 32
+                at = (d * 2 + s) * 128
+                for o in range(4):
+                    low = pl.multiple_of(o * 64 + half * 32, 32)
+                    y_buf[pl.ds(low, 32), at : at + 128] = y[r : r + 32, o * 128 : o * 128 + 128]
+
+    def image_rows(first_depth, depths):
+        at = first_depth * 256
+        t = dot(lift, y_buf[:, at : at + 256 * depths]).astype(BF)
+        for d in range(first_depth, first_depth + depths):
+            for hh in range(10):
+                for od in range(4):
+                    for oh in range(4):
+                        if (d - od) % 2 == 0 and (hh - oh) % 2 == 0:
+                            d2, h2 = (d - od) // 2, (hh - oh) // 2
+                            if 0 <= d2 < 4 and 0 <= h2 < 4:
+                                r = (od * 4 + oh) * 16
+                                for s in range(2):
+                                    to = d2 * 1024 + s * 512 + h2 * 128
+                                    c = ((d - first_depth) * 2 + s) * 128
+                                    i_buf[r : r + 16, to : to + 128] = t[
+                                        hh * 16 : hh * 16 + 16, c : c + 128
+                                    ]
 
     sums["kernel"] = jnp.zeros((128, 256), F32)
     sums["first"] = jnp.zeros((128, 256), F32)
     sums["bias"] = jnp.zeros((128, 128), F32)
 
-    def contract(s, d2):
-        at = (s * 4 + d2) * 512
-        part = slice(at, at + 512)
-        g = g_buf[:, part]
-        pre = ph_buf[:, part].astype(F32)
-        grad = dot(matrix, g).astype(BF).astype(F32)
-        grad = (grad * jnp.where(pre > 0, 1.0, SLOPE)).astype(BF)
-        act = jnp.where(pre > 0, pre, SLOPE * pre).astype(BF)
-        wide = grad.astype(F32)
-        for o in range(0, 512, 128):
-            sums["bias"] = sums["bias"] + wide[:, o : o + 128]
-        sums["kernel"] = sums["kernel"] + dot_nt(act, g)
-        sums["first"] = sums["first"] + dot_nt(grad, i_buf[:, part])
-
-    for s in range(2):
-        gradient_rows(s, (0, 1))
-        gradient_rows(s, (2, 3))
-        for d in range(1, 9):
-            image_rows(s, d)
+    def contract(d2, blocks):
+        for at in range(d2 * 1024, (d2 + blocks) * 1024, 512):
+            part = slice(at, at + 512)
+            pre = ph_buf[:, part].astype(F32)
+            grad = dot(matrix, g_buf[:, part]).astype(BF).astype(F32)
+            grad = (grad * jnp.where(pre > 0, 1.0, SLOPE)).astype(BF)
+            ph_buf[:, part] = jnp.where(pre > 0, pre, SLOPE * pre).astype(BF)
+            f_buf[:, part] = grad
+            wide = grad.astype(F32)
+            for o in range(0, 512, 128):
+                sums["bias"] = sums["bias"] + wide[:, o : o + 128]
+        part = slice(d2 * 1024, (d2 + blocks) * 1024)
+        sums["kernel"] = sums["kernel"] + dot_nt(ph_buf[:, part], g_buf[:, part])
+        sums["first"] = sums["first"] + dot_nt(f_buf[:, part], i_buf[:, part])
+
+    inner = list(range(1, cells + 1))
+    gradient_rows(h, (0, 1, 2, 3))
+    image_shift(h, inner)
+    for c in partner(1 - h):
+        c.wait_recv()
+    gradient_rows(1 - h, (0, 1, 2, 3))
+    image_shift(1 - h, inner)
+    image_rows(1, cells)
 
     @pl.when(k < count - 1)
     def _():
@@ -256,9 +303,7 @@
             c.wait_recv()
             r.start()
 
-    for s in range(2):
-        contract(s, 1)
-        contract(s, 2)
+    contract(1, 2)
 
     @pl.when(k < count - 1)
     def _():
@@ -272,10 +317,11 @@
 
     for s in range(2):
         gradient_rows(s, (4,))
-        image_rows(s, 0)
-        image_rows(s, 9)
-        contract(s, 0)
-        contract(s, 3)
+        image_shift(s, [0, cells + 1])
+    image_rows(0, 1)
+    image_rows(cells + 1, 1)
+    contract(0, 1)
+    contract(3, 1)
 
     deep, first = sums["kernel"], sums["first"]
     blocks = []
@@ -319,16 +365,16 @@
             device_id_type=MESH,
         )
 
-    scatter = [hop(src.at[block(peers[j])], arrived.at[j], 0, j, peers[j]) for j in range(1, members)]
+    scatter = [hop(src.at[block(peers[j])], arrived.at[j], 0, j, peers[j]) for j in turns]
     for c in scatter:
         c.start()
     total = src[block(index), :]
-    for j, c in enumerate(scatter):
+    for j, c in reversed(list(zip(turns, scatter))):
         c.wait_recv()
-        total = total + arrived[j + 1]
+        total = total + arrived[j]
     mine[...] = total
     whole[block(index), :] = total
-    gather = [hop(mine, whole.at[block(index)], 1, j, peers[j]) for j in range(1, members)]
+    gather = [hop(mine, whole.at[block(index)], 1, j, peers[j]) for j in turns]
     for c in gather:
         c.start()
 
@@ -345,8 +391,8 @@
         for c in up() + relay_above(h):
             c.wait_send()
 
-    for j in range(1, members):
-        source = lax.rem(index + members - j, members)
+    for j in turns:
+        source = origin(j)
         hop(mine, whole.at[block(source)], 1, j, source).wait_recv()
     for c in gather:
         c.wait_send()
@@ -360,18 +406,23 @@
     return pl.pallas_call(
         functools.partial(fused_kernel, count, heights),
         out_shape=jax.ShapeDtypeStruct((members * size, 128), F32),
-        in_specs=[vmem()] * 5,
+        in_specs=[pl.BlockSpec(memory_space=pl.ANY)] * 5,
         out_specs=vmem(),
         scratch_shapes=[
+            pltpu.VMEM(hidden.shape, BF),
+            pltpu.VMEM(weight.shape, BF),
             pltpu.VMEM((2, samples, chans, cells + 2, rows, width), BF),
             pltpu.VMEM((2, out_chans, coarse + 1, coarse_rows, coarse_width), BF),
             pltpu.VMEM((2, 2) + pooled.shape, BF),
             pltpu.VMEM((128, 4096), BF),
+            pltpu.VMEM((128, 4096), BF),
             pltpu.VMEM((256, 4096), BF),
+            pltpu.VMEM((256, (cells + 2) * 256), BF),
             pltpu.VMEM((256, 4096), BF),
             pltpu.VMEM((members * size, 128), F32),
             pltpu.VMEM((members, size, 128), F32),
             pltpu.VMEM((size, 128), F32),
+            pltpu.SemaphoreType.DMA((5,)),
             pltpu.SemaphoreType.DMA((11,)),
             pltpu.SemaphoreType.DMA((11,)),
             pltpu.SemaphoreType.DMA((4, members)),

time: 28.1 us -> 26.3 us (0.936)
  Pallas kernels: 27.2 us -> 25.5 us
    pallas_call x1, Pallas kernels: 25.5 us -> 23.8 us  [fused(): pl.pallas_call(functools.partial(fused_kernel, count, heights), out_shape...]
where the time goes in v3:
time: 26.3 us; the launch traced here: 26.1 us
  Pallas kernels  25.5 us (97%)
  between operations  0.64 us (2%)
    pallas_call x1, Pallas kernels, fused(): pl.pallas_call(functools.partial(fused_kernel, count, heights), out_shape...  23.8 us
    pallas_call x1, Pallas kernels, unpack(): pl.pallas_call(unpack_kernel, out_shape=(jax.ShapeDtypeStruct((27, 16, 32...  1.73 us

profile of v3, /device:TPU:0, one launch (start us, length us, event | category | flops | bytes accessed | tf_op | source)
XLA Modules:
  0.0 26.1 jit_solution(1266240968641103585)
XLA Ops:
  0.6 23.8 %shard_map.84.whole = f32[128,128]{1,0:T(8,128)} custom-call(bf16[2,16,8,8,256]{4,3,2,1,0:T(8,128)(2,1)} %hid_in.1, bf16[2,4,8,8,256]{4,3,2,1,0:T(8,128)(2,1)} %img_in.1, bf16[32,4,8,128]{3,2,1,0:T(8,128)(2,1)} %bitcast.13, bf16[32,2,256]{2,1,0:T(2,128)(2,1)} %bitcast.15, bf16[27,16,32]{2,1,0:T(8,128)(2,1)} %bitcast.14), custom_call_target="tpu_custom_call" | custom-call | tf_op jit(solution)/shard_map/pallas_call | solution.py:406
  24.4 1.7 %shard_map.85 = (f32[27,16,32]{2,1,0:T(8,128)}, f32[27,4,16]{2,1,0:T(4,128)}, f32[1,32]{1,0:T(1,128)}, f32[1,16]{1,0:T(1,128)}) custom-call(f32[128,128]{1,0:T(8,128)} %shard_map.84.whole), custom_call_target="tpu_custom_call" | custom-call | tf_op jit(solution)/shard_map/pallas_call | solution.py:448

commit v4 on v3

--- a/solution.py
+++ b/solution.py
@@ -372,9 +372,9 @@
     for j, c in reversed(list(zip(turns, scatter))):
         c.wait_recv()
         total = total + arrived[j]
-    mine[...] = total
-    whole[block(index), :] = total
-    gather = [hop(mine, whole.at[block(index)], 1, j, peers[j]) for j in turns]
+    mine[...] = total.astype(BF)
+    whole[index] = total.astype(BF)
+    gather = [hop(mine, whole.at[index], 1, j, peers[j]) for j in turns]
     for c in gather:
         c.start()
 
@@ -393,7 +393,7 @@
 
     for j in turns:
         source = origin(j)
-        hop(mine, whole.at[block(source)], 1, j, source).wait_recv()
+        hop(mine, whole.at[source], 1, j, source).wait_recv()
     for c in gather:
         c.wait_send()
 
@@ -405,7 +405,7 @@
     size = 8 * (-(-128 // (8 * members)))
     return pl.pallas_call(
         functools.partial(fused_kernel, count, heights),
-        out_shape=jax.ShapeDtypeStruct((members * size, 128), F32),
+        out_shape=jax.ShapeDtypeStruct((members, size, 128), BF),
         in_specs=[pl.BlockSpec(memory_space=pl.ANY)] * 5,
         out_specs=vmem(),
         scratch_shapes=[
@@ -421,7 +421,7 @@
             pltpu.VMEM((256, 4096), BF),
             pltpu.VMEM((members * size, 128), F32),
             pltpu.VMEM((members, size, 128), F32),
-            pltpu.VMEM((size, 128), F32),
+            pltpu.VMEM((size, 128), BF),
             pltpu.SemaphoreType.DMA((5,)),
             pltpu.SemaphoreType.DMA((11,)),
             pltpu.SemaphoreType.DMA((11,)),
@@ -431,7 +431,8 @@
     )(hidden, images, pre_deep, pooled, weight)
 
 
-def unpack_kernel(whole, deep, first, deep_bias, first_bias):
+def unpack_kernel(gathered, deep, first, deep_bias, first_bias):
+    whole = gathered[...].astype(F32).reshape(-1, 128)
     for t in range(27):
         r, c = (t // 4) * 16, (t % 4) * 32
         deep[t] = whole[r : r + 16, c : c + 32]

time: 26.3 us -> 26.2 us (level)
  no operation moved by 1% of the time
where the time goes in v4:
time: 26.2 us; the launch traced here: 26 us
  Pallas kernels  25.3 us (97%)
  between operations  0.64 us (2%)
    pallas_call x1, Pallas kernels, fused(): pl.pallas_call(functools.partial(fused_kernel, count, heights), out_shape...  23.7 us
    pallas_call x1, Pallas kernels, unpack(): pl.pallas_call(unpack_kernel, out_shape=(jax.ShapeDtypeStruct((27, 16, 32...  1.6 us

profile of v4, /device:TPU:0, one launch (start us, length us, event | category | flops | bytes accessed | tf_op | source)
XLA Modules:
  0.0 26.0 jit_solution(8677482433960171552)
XLA Ops:
  0.6 23.7 %shard_map.84.gathered = bf16[16,8,128]{2,1,0:T(8,128)(2,1)} custom-call(bf16[2,16,8,8,256]{4,3,2,1,0:T(8,128)(2,1)} %hid_in.1, bf16[2,4,8,8,256]{4,3,2,1,0:T(8,128)(2,1)} %img_in.1, bf16[32,4,8,128]{3,2,1,0:T(8,128)(2,1)} %bitcast.13, bf16[32,2,256]{2,1,0:T(2,128)(2,1)} %bitcast.15, bf16[27,16,32]{2,1,0:T(8,128)(2,1)} %bitcast.14), custom_call_target="tpu_custom_call" | custom-call | tf_op jit(solution)/shard_map/pallas_call | solution.py:406
  24.4 1.6 %shard_map.85 = (f32[27,16,32]{2,1,0:T(8,128)}, f32[27,4,16]{2,1,0:T(4,128)}, f32[1,32]{1,0:T(1,128)}, f32[1,16]{1,0:T(1,128)}) custom-call(bf16[16,8,128]{2,1,0:T(8,128)(2,1)} %shard_map.84.gathered), custom_call_target="tpu_custom_call" | custom-call | tf_op jit(solution)/shard_map/pallas_call | solution.py:449
